TPU v7x, 32 devices: a whole 2x2x4 slice. The times are simulated.
32 devices in a mesh: rows: 8 (over z, y), cols: 4 (over x, core).
Axes of the slice: x: 2, y: 2, z: 4, core: 2. Of those that a mesh axis runs over, the one named last changes fastest.
Arguments:
- start_panel: float32 [64, 16384], P(None, ('rows', 'cols')), may hold values from -6 to 6
- tile_values: float32 [128, 16, 128, 128], P('rows', 'cols')
- tile_column: int32 [128, 16], P('rows', 'cols'), may hold values from 0 to 127, as said below
- tile_count: int32 [128], P('rows'), may hold values from 8 to 16, as said below
Outputs:
- basis: float32 [64, 16384], P(None, ('rows', 'cols'))
Inputs may be any that keep to these rules, and one draw needn't show every extreme that they name: `tile_count`: every row block has between half of its slots and all 16 slots live; some row block has all 16 live. `tile_column`: in row block i the entries are distinct column blocks, each within 16 blocks of i, and the first is i itself; slots at or beyond tile_count[i] hold such entries too but are not used.
All inputs are finite; a program needn't handle non-finite values.
Results may differ from a plain program's by a relative error of at most 0.0003.
Values sent between devices are 32-bit elements; how exact they have to be, the bound alone decides.
A program may use at most 64 MiB of HBM per device.

v0:
```python
import math
import jax
import jax.numpy as jnp
from jax import lax
from jax.sharding import PartitionSpec as P

ITERS = 3


def with_halo(block, sides, width):
    for axis, dim in sides:
        count = lax.axis_size(axis)
        forward = [(i, i + 1) for i in range(count - 1)]
        backward = [(target, source) for source, target in forward]
        low = lax.ppermute(
            lax.slice_in_dim(block, block.shape[dim] - width, None, axis=dim), axis, forward
        )
        high = lax.ppermute(lax.slice_in_dim(block, 0, width, axis=dim), axis, backward)
        block = jnp.concatenate([low, block, high], axis=dim)
    return block


def local_product(extended, tile_values, tile_column, tile_count):
    owned_blocks = tile_values.shape[0]
    slot_dev = tile_values.shape[1]
    tile_width = tile_values.shape[2]
    anchor = lax.axis_index("rows") * owned_blocks - owned_blocks
    local_column = tile_column - anchor
    blocks = extended.reshape(extended.shape[0], 3 * owned_blocks, tile_width)
    picked = jnp.take(blocks, local_column, axis=1)
    slot_ids = lax.axis_index("cols") * slot_dev + jnp.arange(slot_dev, dtype=jnp.int32)
    alive_mask = slot_ids[None, :] < tile_count[:, None]
    picked = jnp.where(alive_mask[None, :, :, None], picked, jnp.float32(0.0))
    result = jnp.einsum("disk,isnk->din", picked, tile_values, precision=lax.Precision.HIGHEST)
    return result.reshape(extended.shape[0], owned_blocks * tile_width)


def per_device(start_panel, tile_values, tile_column, tile_count):

    def fetch_owner(panel_part):
        return lax.all_gather(panel_part, "cols", axis=1, tiled=True)

    def partial_of(owner_panel):
        extended = with_halo(owner_panel, (("rows", 1),), owner_panel.shape[1])
        return local_product(extended, tile_values, tile_column, tile_count)

    def reduce_share(partial_terms):
        return lax.psum_scatter(partial_terms, "cols", scatter_dimension=1, tiled=True)

    panel = start_panel
    for sweep_index in range(ITERS):
        first_terms = partial_of(fetch_owner(panel))
        middle = fetch_owner(reduce_share(first_terms))
        second = reduce_share(partial_of(middle))
        local_gram = jnp.dot(
            second, second.T, precision=lax.Precision.HIGHEST, preferred_element_type=jnp.float32
        )
        lower_factor = jnp.linalg.cholesky(lax.psum(local_gram, ("rows", "cols")))
        panel = lax.linalg.triangular_solve(lower_factor, second, left_side=True, lower=True)
    scaling = math.sqrt(lax.axis_size("rows") * lax.axis_size("cols") * panel.shape[1])
    return panel * jnp.float32(scaling)


def solution(mesh):
    in_specs = (
        P(None, ("rows", "cols")),
        P("rows", "cols", None, None),
        P("rows", "cols"),
        P("rows"),
    )
    out_specs = P(None, ("rows", "cols"))
    return jax.shard_map(
        per_device, mesh=mesh, in_specs=in_specs, out_specs=out_specs, check_vma=False
    )
```

profile of v0, /device:TPU:0, one launch (start us, length us, event | category | flops | bytes accessed | tf_op | source)
XLA Modules:
  0.0 582.8 jit_solution(2102967249004942591)
XLA Ops:
  6.5 8.8 %all_gather.18 = f32[64,2048]{1,0:T(8,128)S(1)} all-gather(f32[64,512]{1,0:T(8,128)} %param.9), channel_id=1, replica_groups=mesh['rows'=8,'cols'=4] {'cols'}, dimensions={1}, use_global_device_ids=true | all-gather | bytes 655360 | tf_op jit(solution)/shard_map/all_gather | solution.py:41
  16.6 4.6 collective-permute-start
  23.0 8.5 %collective-permute-done.1 = f32[64,2048]{1,0:T(8,128)S(1)} collective-permute-done((f32[64,2048]{1,0:T(8,128)S(1)}, f32[64,2048]{1,0:T(8,128)S(1)}, u32[]{:S(2)}, u32[]{:S(2)}) %collective-permute-start.1) | collective-permute-done | bytes 524320 | tf_op jit(solution)/shard_map/ppermute | solution.py:18
  31.4 11.2 %collective-permute-done = f32[64,2048]{1,0:T(8,128)S(1)} collective-permute-done((f32[64,2048]{1,0:T(8,128)S(1)}, f32[64,2048]{1,0:T(8,128)S(1)}, u32[]{:S(2)}, u32[]{:S(2)}) %collective-permute-start) | collective-permute-done | bytes 524320 | tf_op jit(solution)/shard_map/ppermute | solution.py:15
  42.8 2.0 gather_fusion
  44.8 7.4 %fusion.12 = f32[16,8,8,128]{3,2,1,0:T(8,128)S(1)} fusion(f32[16,4,128,128]{3,2,1,0:T(8,128)} %param.10, f32[16,4,64,128]{3,2,1,0:T(8,128)} %bitcast.163, pred[16,4]{1,0:T(8,128)(4,1)S(1)} %copy.52, pred[16,4]{1,0:T(8,128)(4,1)S(1)} %broadcast_compare_fusion), kind=kOutput, calls=%fused_computation.36 | convolution fusion | flops 806354944 | bytes 6815872 | tf_op jit(solution)/shard_map/disk,isnk->din/dot_general | solution.py:34
  53.2 22.6 %reduce-scatter.7.cloned.1.call-done = f32[64,512]{1,0:T(8,128)} async-done(((f32[64,2048]{1,0:T(8,128)}), f32[64,512]{1,0:T(8,128)}) %reduce-scatter.7.cloned.1.call-update) | async-done | bytes 131088 | tf_op jit(solution)/shard_map/reduce_scatter | solution.py:48
  75.7 7.0 %all_gather.19 = f32[64,2048]{1,0:T(8,128)S(1)} all-gather(f32[64,512]{1,0:T(8,128)} %reduce-scatter.7.cloned.1.call-done), channel_id=1, replica_groups=mesh['rows'=8,'cols'=4] {'cols'}, dimensions={1}, use_global_device_ids=true | all-gather | bytes 655360 | tf_op jit(solution)/shard_map/all_gather | solution.py:41
  84.0 4.6 collective-permute-start.2
  88.6 10.2 %collective-permute-done.3 = f32[64,2048]{1,0:T(8,128)S(1)} collective-permute-done((f32[64,2048]{1,0:T(8,128)S(1)}, f32[64,2048]{1,0:T(8,128)S(1)}, u32[]{:S(2)}, u32[]{:S(2)}) %collective-permute-start.3) | collective-permute-done | bytes 524320 | tf_op jit(solution)/shard_map/ppermute | solution.py:18
  98.8 11.1 %collective-permute-done.2 = f32[64,2048]{1,0:T(8,128)S(1)} collective-permute-done((f32[64,2048]{1,0:T(8,128)S(1)}, f32[64,2048]{1,0:T(8,128)S(1)}, u32[]{:S(2)}, u32[]{:S(2)}) %collective-permute-start.2) | collective-permute-done | bytes 524320 | tf_op jit(solution)/shard_map/ppermute | solution.py:15
  112.1 7.4 %fusion.13 = f32[16,8,8,128]{3,2,1,0:T(8,128)S(1)} fusion(f32[16,4,128,128]{3,2,1,0:T(8,128)} %param.10, f32[16,4,64,128]{3,2,1,0:T(8,128)} %bitcast.164, pred[16,4]{1,0:T(8,128)(4,1)S(1)} %copy.52, pred[16,4]{1,0:T(8,128)(4,1)S(1)} %broadcast_compare_fusion), kind=kOutput, calls=%fused_computation.37 | convolution fusion | flops 806354944 | bytes 6815872 | tf_op jit(solution)/shard_map/disk,isnk->din/dot_general | solution.py:34
  120.5 22.2 %reduce-scatter.9.cloned.1.call-done = f32[64,512]{1,0:T(8,128)} async-done(((f32[64,2048]{1,0:T(8,128)}), f32[64,512]{1,0:T(8,128)}) %reduce-scatter.9.cloned.1.call-update) | async-done | bytes 131088 | tf_op jit(solution)/shard_map/reduce_scatter | solution.py:48
  143.9 39.7 %psum.21 = f32[64,64]{0,1:T(8,128)S(1)} all-reduce(f32[64,64]{0,1:T(8,128)S(1)} %fusion.69), channel_id=1, replica_groups=mesh['rows'=8,'cols'=4] {'rows','cols'}, use_global_device_ids=true, to_apply=%region_2.4 | all-reduce | flops 4096 | bytes 32768 | tf_op jit(solution)/shard_map/psum | solution.py:58
  183.7 5.8 %cholesky.59 = f32[64,64]{1,0:T(8,128)S(1)} custom-call(f32[64,64]{1,0:T(8,128)S(1)} %fusion.52), custom_call_target="Cholesky" | custom-call | tf_op jit(solution)/shard_map/jit(cholesky)/cholesky | solution.py:58
  190.8 4.9 custom-call.7
  197.0 7.9 %all_gather.20 = f32[64,2048]{1,0:T(8,128)S(1)} all-gather(f32[64,512]{1,0:T(8,128)S(1)} %fusion.50), channel_id=1, replica_groups=mesh['rows'=8,'cols'=4] {'cols'}, dimensions={1}, use_global_device_ids=true | all-gather | bytes 655360 | tf_op jit(solution)/shard_map/all_gather | solution.py:41
  206.2 4.6 collective-permute-start.4
  210.8 10.2 %collective-permute-done.5 = f32[64,2048]{1,0:T(8,128)S(1)} collective-permute-done((f32[64,2048]{1,0:T(8,128)S(1)}, f32[64,2048]{1,0:T(8,128)S(1)}, u32[]{:S(2)}, u32[]{:S(2)}) %collective-permute-start.5) | collective-permute-done | bytes 524320 | tf_op jit(solution)/shard_map/ppermute | solution.py:18
  221.0 11.2 %collective-permute-done.4 = f32[64,2048]{1,0:T(8,128)S(1)} collective-permute-done((f32[64,2048]{1,0:T(8,128)S(1)}, f32[64,2048]{1,0:T(8,128)S(1)}, u32[]{:S(2)}, u32[]{:S(2)}) %collective-permute-start.4) | collective-permute-done | bytes 524320 | tf_op jit(solution)/shard_map/ppermute | solution.py:15
  232.3 2.0 gather_fusion.2
  234.4 7.4 %fusion.14 = f32[16,8,8,128]{3,2,1,0:T(8,128)S(1)} fusion(f32[16,4,128,128]{3,2,1,0:T(8,128)} %param.10, f32[16,4,64,128]{3,2,1,0:T(8,128)} %bitcast.165, pred[16,4]{1,0:T(8,128)(4,1)S(1)} %copy.52, pred[16,4]{1,0:T(8,128)(4,1)S(1)} %broadcast_compare_fusion), kind=kOutput, calls=%fused_computation.38 | convolution fusion | flops 806354944 | bytes 6815872 | tf_op jit(solution)/shard_map/disk,isnk->din/dot_general | solution.py:34
  242.7 22.1 %reduce-scatter.11.cloned.1.call-done = f32[64,512]{1,0:T(8,128)} async-done(((f32[64,2048]{1,0:T(8,128)}), f32[64,512]{1,0:T(8,128)}) %reduce-scatter.11.cloned.1.call-update) | async-done | bytes 131088 | tf_op jit(solution)/shard_map/reduce_scatter | solution.py:48
  264.8 7.0 %all_gather.21 = f32[64,2048]{1,0:T(8,128)S(1)} all-gather(f32[64,512]{1,0:T(8,128)} %reduce-scatter.11.cloned.1.call-done), channel_id=1, replica_groups=mesh['rows'=8,'cols'=4] {'cols'}, dimensions={1}, use_global_device_ids=true | all-gather | bytes 655360 | tf_op jit(solution)/shard_map/all_gather | solution.py:41
  273.1 4.6 collective-permute-start.6
  277.7 10.2 %collective-permute-done.7 = f32[64,2048]{1,0:T(8,128)S(1)} collective-permute-done((f32[64,2048]{1,0:T(8,128)S(1)}, f32[64,2048]{1,0:T(8,128)S(1)}, u32[]{:S(2)}, u32[]{:S(2)}) %collective-permute-start.7) | collective-permute-done | bytes 524320 | tf_op jit(solution)/shard_map/ppermute | solution.py:18
  287.9 11.1 %collective-permute-done.6 = f32[64,2048]{1,0:T(8,128)S(1)} collective-permute-done((f32[64,2048]{1,0:T(8,128)S(1)}, f32[64,2048]{1,0:T(8,128)S(1)}, u32[]{:S(2)}, u32[]{:S(2)}) %collective-permute-start.6) | collective-permute-done | bytes 524320 | tf_op jit(solution)/shard_map/ppermute | solution.py:15
  299.2 2.0 gather_fusion.3
  301.2 7.4 %fusion.15 = f32[16,8,8,128]{3,2,1,0:T(8,128)S(1)} fusion(f32[16,4,128,128]{3,2,1,0:T(8,128)} %param.10, f32[16,4,64,128]{3,2,1,0:T(8,128)} %bitcast.166, pred[16,4]{1,0:T(8,128)(4,1)S(1)} %copy.52, pred[16,4]{1,0:T(8,128)(4,1)S(1)} %broadcast_compare_fusion), kind=kOutput, calls=%fused_computation.39 | convolution fusion | flops 806354944 | bytes 6815872 | tf_op jit(solution)/shard_map/disk,isnk->din/dot_general | solution.py:34
  309.6 22.2 %reduce-scatter.13.cloned.1.call-done = f32[64,512]{1,0:T(8,128)} async-done(((f32[64,2048]{1,0:T(8,128)}), f32[64,512]{1,0:T(8,128)}) %reduce-scatter.13.cloned.1.call-update) | async-done | bytes 131088 | tf_op jit(solution)/shard_map/reduce_scatter | solution.py:48
  333.0 39.7 %psum.22 = f32[64,64]{0,1:T(8,128)S(1)} all-reduce(f32[64,64]{0,1:T(8,128)S(1)} %fusion.70), channel_id=1, replica_groups=mesh['rows'=8,'cols'=4] {'rows','cols'}, use_global_device_ids=true, to_apply=%region_7.11 | all-reduce | flops 4096 | bytes 32768 | tf_op jit(solution)/shard_map/psum | solution.py:58
  372.8 5.8 %cholesky.70 = f32[64,64]{1,0:T(8,128)S(1)} custom-call(f32[64,64]{1,0:T(8,128)S(1)} %fusion.49), custom_call_target="Cholesky" | custom-call | tf_op jit(solution)/shard_map/jit(cholesky)/cholesky | solution.py:58
  380.0 4.9 custom-call.8
  386.1 7.9 %all_gather.22 = f32[64,2048]{1,0:T(8,128)S(1)} all-gather(f32[64,512]{1,0:T(8,128)S(1)} %fusion.47), channel_id=1, replica_groups=mesh['rows'=8,'cols'=4] {'cols'}, dimensions={1}, use_global_device_ids=true | all-gather | bytes 655360 | tf_op jit(solution)/shard_map/all_gather | solution.py:41
  395.4 4.6 collective-permute-start.8
  400.0 10.2 %collective-permute-done.9 = f32[64,2048]{1,0:T(8,128)S(1)} collective-permute-done((f32[64,2048]{1,0:T(8,128)S(1)}, f32[64,2048]{1,0:T(8,128)S(1)}, u32[]{:S(2)}, u32[]{:S(2)}) %collective-permute-start.9) | collective-permute-done | bytes 524320 | tf_op jit(solution)/shard_map/ppermute | solution.py:18
  410.1 11.2 %collective-permute-done.8 = f32[64,2048]{1,0:T(8,128)S(1)} collective-permute-done((f32[64,2048]{1,0:T(8,128)S(1)}, f32[64,2048]{1,0:T(8,128)S(1)}, u32[]{:S(2)}, u32[]{:S(2)}) %collective-permute-start.8) | collective-permute-done | bytes 524320 | tf_op jit(solution)/shard_map/ppermute | solution.py:15
  423.6 7.4 %fusion.16 = f32[16,8,8,128]{3,2,1,0:T(8,128)S(1)} fusion(f32[16,4,128,128]{3,2,1,0:T(8,128)} %param.10, f32[16,4,64,128]{3,2,1,0:T(8,128)} %bitcast.167, pred[16,4]{1,0:T(8,128)(4,1)S(1)} %copy.52, pred[16,4]{1,0:T(8,128)(4,1)S(1)} %broadcast_compare_fusion), kind=kOutput, calls=%fused_computation.40 | convolution fusion | flops 806354944 | bytes 6815872 | tf_op jit(solution)/shard_map/disk,isnk->din/dot_general | solution.py:34
  431.9 22.0 %reduce-scatter.15.cloned.1.call-done = f32[64,512]{1,0:T(8,128)} async-done(((f32[64,2048]{1,0:T(8,128)}), f32[64,512]{1,0:T(8,128)}) %reduce-scatter.15.cloned.1.call-update) | async-done | bytes 131088 | tf_op jit(solution)/shard_map/reduce_scatter | solution.py:48
  453.9 7.0 %all_gather.23 = f32[64,2048]{1,0:T(8,128)S(1)} all-gather(f32[64,512]{1,0:T(8,128)} %reduce-scatter.15.cloned.1.call-done), channel_id=1, replica_groups=mesh['rows'=8,'cols'=4] {'cols'}, dimensions={1}, use_global_device_ids=true | all-gather | bytes 655360 | tf_op jit(solution)/shard_map/all_gather | solution.py:41
  462.2 4.6 collective-permute-start.10
  466.8 10.2 %collective-permute-done.11 = f32[64,2048]{1,0:T(8,128)S(1)} collective-permute-done((f32[64,2048]{1,0:T(8,128)S(1)}, f32[64,2048]{1,0:T(8,128)S(1)}, u32[]{:S(2)}, u32[]{:S(2)}) %collective-permute-start.11) | collective-permute-done | bytes 524320 | tf_op jit(solution)/shard_map/ppermute | solution.py:18
  477.0 11.1 %collective-permute-done.10 = f32[64,2048]{1,0:T(8,128)S(1)} collective-permute-done((f32[64,2048]{1,0:T(8,128)S(1)}, f32[64,2048]{1,0:T(8,128)S(1)}, u32[]{:S(2)}, u32[]{:S(2)}) %collective-permute-start.10) | collective-permute-done | bytes 524320 | tf_op jit(solution)/shard_map/ppermute | solution.py:15
  490.3 7.4 %fusion.17 = f32[16,8,8,128]{3,2,1,0:T(8,128)S(1)} fusion(f32[16,4,128,128]{3,2,1,0:T(8,128)} %param.10, f32[16,4,64,128]{3,2,1,0:T(8,128)} %bitcast.162, pred[16,4]{1,0:T(8,128)(4,1)S(1)} %copy.52, pred[16,4]{1,0:T(8,128)(4,1)S(1)} %broadcast_compare_fusion), kind=kOutput, calls=%fused_computation.41 | convolution fusion | flops 806354944 | bytes 6815872 | tf_op jit(solution)/shard_map/disk,isnk->din/dot_general | solution.py:34
  498.6 22.3 %reduce-scatter.17.cloned.1.call-done = f32[64,512]{1,0:T(8,128)} async-done(((f32[64,2048]{1,0:T(8,128)}), f32[64,512]{1,0:T(8,128)}) %reduce-scatter.17.cloned.1.call-update) | async-done | bytes 131088 | tf_op jit(solution)/shard_map/reduce_scatter | solution.py:48
  522.1 39.8 %psum.23 = f32[64,64]{0,1:T(8,128)S(1)} all-reduce(f32[64,64]{0,1:T(8,128)S(1)} %fusion.71), channel_id=1, replica_groups=mesh['rows'=8,'cols'=4] {'rows','cols'}, use_global_device_ids=true, to_apply=%region_10.14 | all-reduce | flops 4096 | bytes 32768 | tf_op jit(solution)/shard_map/psum | solution.py:58
  562.0 5.8 %cholesky.81 = f32[64,64]{1,0:T(8,128)S(1)} custom-call(f32[64,64]{1,0:T(8,128)S(1)} %fusion.46), custom_call_target="Cholesky" | custom-call | tf_op jit(solution)/shard_map/jit(cholesky)/cholesky | solution.py:58
  569.2 4.9 custom-call.9
  (61 shorter events, 34.2 us)
Async XLA Ops:
  6.5 69.2 %reduce-scatter.7.cloned.1.call-start = ((), (), s32[]{:S(2)}) async-start(), calls=%async_computation.6 | async-start | bytes 655360 | tf_op jit(solution)/shard_map/reduce_scatter | solution.py:48
  15.4 16.1 %collective-permute-start.1 = (f32[64,2048]{1,0:T(8,128)S(1)}, f32[64,2048]{1,0:T(8,128)S(1)}, u32[]{:S(2)}, u32[]{:S(2)}) collective-permute-start(f32[64,2048]{1,0:T(8,128)S(1)} %all_gather.18), channel_id=1, source_target_pairs={{4,0},{8,4},{12,8},{16,12},{20,16},{24,20},{28,24},{5,1},{9,5},{13... | collective-permute-start | bytes 1572872 | tf_op jit(solution)/shard_map/ppermute | solution.py:18
  16.6 25.9 %collective-permute-start = (f32[64,2048]{1,0:T(8,128)S(1)}, f32[64,2048]{1,0:T(8,128)S(1)}, u32[]{:S(2)}, u32[]{:S(2)}) collective-permute-start(f32[64,2048]{1,0:T(8,128)S(1)} %all_gather.18), channel_id=1, source_target_pairs={{0,4},{4,8},{8,12},{12,16},{16,20},{20,24},{24,28},{1,5},{5,9},{9,... | collective-permute-start | bytes 1572872 | tf_op jit(solution)/shard_map/ppermute | solution.py:15
  53.1 89.5 %reduce-scatter.9.cloned.1.call-start = ((), (), s32[]{:S(2)}) async-start(), calls=%async_computation.7 | async-start | bytes 655360 | tf_op jit(solution)/shard_map/reduce_scatter | solution.py:48
  82.7 16.1 %collective-permute-start.3 = (f32[64,2048]{1,0:T(8,128)S(1)}, f32[64,2048]{1,0:T(8,128)S(1)}, u32[]{:S(2)}, u32[]{:S(2)}) collective-permute-start(f32[64,2048]{1,0:T(8,128)S(1)} %all_gather.19), channel_id=1, source_target_pairs={{4,0},{8,4},{12,8},{16,12},{20,16},{24,20},{28,24},{5,1},{9,5},{13... | collective-permute-start | bytes 1572872 | tf_op jit(solution)/shard_map/ppermute | solution.py:18
  84.0 25.9 %collective-permute-start.2 = (f32[64,2048]{1,0:T(8,128)S(1)}, f32[64,2048]{1,0:T(8,128)S(1)}, u32[]{:S(2)}, u32[]{:S(2)}) collective-permute-start(f32[64,2048]{1,0:T(8,128)S(1)} %all_gather.19), channel_id=1, source_target_pairs={{0,4},{4,8},{8,12},{12,16},{16,20},{20,24},{24,28},{1,5},{5,9},{9,... | collective-permute-start | bytes 1572872 | tf_op jit(solution)/shard_map/ppermute | solution.py:15
  120.4 144.4 %reduce-scatter.11.cloned.1.call-start = ((), (), s32[]{:S(2)}) async-start(), calls=%async_computation.8 | async-start | bytes 655360 | tf_op jit(solution)/shard_map/reduce_scatter | solution.py:48
  204.9 16.1 %collective-permute-start.5 = (f32[64,2048]{1,0:T(8,128)S(1)}, f32[64,2048]{1,0:T(8,128)S(1)}, u32[]{:S(2)}, u32[]{:S(2)}) collective-permute-start(f32[64,2048]{1,0:T(8,128)S(1)} %all_gather.20), channel_id=1, source_target_pairs={{4,0},{8,4},{12,8},{16,12},{20,16},{24,20},{28,24},{5,1},{9,5},{13... | collective-permute-start | bytes 1572872 | tf_op jit(solution)/shard_map/ppermute | solution.py:18
  206.2 25.9 %collective-permute-start.4 = (f32[64,2048]{1,0:T(8,128)S(1)}, f32[64,2048]{1,0:T(8,128)S(1)}, u32[]{:S(2)}, u32[]{:S(2)}) collective-permute-start(f32[64,2048]{1,0:T(8,128)S(1)} %all_gather.20), channel_id=1, source_target_pairs={{0,4},{4,8},{8,12},{12,16},{16,20},{20,24},{24,28},{1,5},{5,9},{9,... | collective-permute-start | bytes 1572872 | tf_op jit(solution)/shard_map/ppermute | solution.py:15
  242.7 89.1 %reduce-scatter.13.cloned.1.call-start = ((), (), s32[]{:S(2)}) async-start(), calls=%async_computation.9 | async-start | bytes 655360 | tf_op jit(solution)/shard_map/reduce_scatter | solution.py:48
  271.8 16.1 %collective-permute-start.7 = (f32[64,2048]{1,0:T(8,128)S(1)}, f32[64,2048]{1,0:T(8,128)S(1)}, u32[]{:S(2)}, u32[]{:S(2)}) collective-permute-start(f32[64,2048]{1,0:T(8,128)S(1)} %all_gather.21), channel_id=1, source_target_pairs={{4,0},{8,4},{12,8},{16,12},{20,16},{24,20},{28,24},{5,1},{9,5},{13... | collective-permute-start | bytes 1572872 | tf_op jit(solution)/shard_map/ppermute | solution.py:18
  273.1 25.9 %collective-permute-start.6 = (f32[64,2048]{1,0:T(8,128)S(1)}, f32[64,2048]{1,0:T(8,128)S(1)}, u32[]{:S(2)}, u32[]{:S(2)}) collective-permute-start(f32[64,2048]{1,0:T(8,128)S(1)} %all_gather.21), channel_id=1, source_target_pairs={{0,4},{4,8},{8,12},{12,16},{16,20},{20,24},{24,28},{1,5},{5,9},{9,... | collective-permute-start | bytes 1572872 | tf_op jit(solution)/shard_map/ppermute | solution.py:15
  309.5 144.4 %reduce-scatter.15.cloned.1.call-start = ((), (), s32[]{:S(2)}) async-start(), calls=%async_computation.10 | async-start | bytes 655360 | tf_op jit(solution)/shard_map/reduce_scatter | solution.py:48
  394.1 16.1 %collective-permute-start.9 = (f32[64,2048]{1,0:T(8,128)S(1)}, f32[64,2048]{1,0:T(8,128)S(1)}, u32[]{:S(2)}, u32[]{:S(2)}) collective-permute-start(f32[64,2048]{1,0:T(8,128)S(1)} %all_gather.22), channel_id=1, source_target_pairs={{4,0},{8,4},{12,8},{16,12},{20,16},{24,20},{28,24},{5,1},{9,5},{13... | collective-permute-start | bytes 1572872 | tf_op jit(solution)/shard_map/ppermute | solution.py:18
  395.4 26.0 %collective-permute-start.8 = (f32[64,2048]{1,0:T(8,128)S(1)}, f32[64,2048]{1,0:T(8,128)S(1)}, u32[]{:S(2)}, u32[]{:S(2)}) collective-permute-start(f32[64,2048]{1,0:T(8,128)S(1)} %all_gather.22), channel_id=1, source_target_pairs={{0,4},{4,8},{8,12},{12,16},{16,20},{20,24},{24,28},{1,5},{5,9},{9,... | collective-permute-start | bytes 1572872 | tf_op jit(solution)/shard_map/ppermute | solution.py:15
  431.9 89.0 %reduce-scatter.17.cloned.1.call-start = ((), (), s32[]{:S(2)}) async-start(), calls=%async_computation.11 | async-start | bytes 655360 | tf_op jit(solution)/shard_map/reduce_scatter | solution.py:48
  460.9 16.1 %collective-permute-start.11 = (f32[64,2048]{1,0:T(8,128)S(1)}, f32[64,2048]{1,0:T(8,128)S(1)}, u32[]{:S(2)}, u32[]{:S(2)}) collective-permute-start(f32[64,2048]{1,0:T(8,128)S(1)} %all_gather.23), channel_id=1, source_target_pairs={{4,0},{8,4},{12,8},{16,12},{20,16},{24,20},{28,24},{5,1},{9,5},{13... | collective-permute-start | bytes 1572872 | tf_op jit(solution)/shard_map/ppermute | solution.py:18
  462.2 25.9 %collective-permute-start.10 = (f32[64,2048]{1,0:T(8,128)S(1)}, f32[64,2048]{1,0:T(8,128)S(1)}, u32[]{:S(2)}, u32[]{:S(2)}) collective-permute-start(f32[64,2048]{1,0:T(8,128)S(1)} %all_gather.23), channel_id=1, source_target_pairs={{0,4},{4,8},{8,12},{12,16},{16,20},{20,24},{24,28},{1,5},{5,9},{9,... | collective-permute-start | bytes 1572872 | tf_op jit(solution)/shard_map/ppermute | solution.py:15
Sparse Core Ops, SparseCore 0:
  53.2 22.4 reduce-scatter.6
  120.5 22.0 reduce-scatter.8
  242.8 21.9 reduce-scatter.10
  309.6 22.0 reduce-scatter.12
  432.0 21.9 reduce-scatter.14
  498.7 22.0 reduce-scatter.16
where the time goes:
time: 584 us; the launch traced here: 583 us
  waiting for transfers between devices  260 us (45%)
  blocking collectives  165 us (28%)
  matrix products  52.7 us (9%)
  other arithmetic  38.8 us (7%)
  starting transfers between devices  35.4 us (6%)
  local copies, waits for them, and re-layouts  17.7 us (3%)
  between operations  13.8 us (2%)
    reduce_scatter x6, waiting for transfers between devices, reduce_share(): lax.psum_scatter(partial_terms, 'cols', scatter_dimension=1, tiled=True)  133 us
    psum x3, blocking collectives, per_device(): lower_factor = jnp.linalg.cholesky(lax.psum(local_gram, ('rows', 'cols')))  119 us
    ppermute x6, waiting for transfers between devices, with_halo(): lax.ppermute(lax.slice_in_dim(block, block.shape[dim] - width, None, axis...  66.9 us
    ppermute x6, waiting for transfers between devices, with_halo(): lax.ppermute(lax.slice_in_dim(block, 0, width, axis=dim), axis, backward)  59.4 us
    all_gather x6, blocking collectives, fetch_owner(): return lax.all_gather(panel_part, 'cols', axis=1, tiled=True)  45.6 us
    dot_general x6, matrix products, local_product(): jnp.einsum('disk,isnk->din', picked, tile_values, precision=lax.Precision...  44.6 us
    ppermute x6, starting transfers between devices, with_halo(): lax.ppermute(lax.slice_in_dim(block, block.shape[dim] - width, None, axis...  27.5 us
    another operation x9, other arithmetic, per_device(): lower_factor = jnp.linalg.cholesky(lax.psum(local_gram, ('rows', 'cols')))  19.6 us
  transfers between devices with their start and end apart: 18, of which 18 were waited for; matrix products, arithmetic and copies ran while one was open for 0% of the time, Pallas kernels for 0%

commit v1 on v0

--- a/solution.py
+++ b/solution.py
@@ -5,6 +5,22 @@
 from jax.sharding import PartitionSpec as P
 
 ITERS = 3
+
+
+def gather_around(x, axis, dim):
+    ways, here, hop = (lax.axis_size(axis), lax.axis_index(axis), x.shape[dim])
+    lengths = [n * ways if d == dim else n for d, n in enumerate(x.shape)]
+    full = lax.dynamic_update_slice_in_dim(jnp.zeros(lengths, x.dtype), x, here * hop, axis=dim)
+    going_up = going_down = x
+    for far in range(1, ways // 2 + 1):
+        going_up = lax.ppermute(going_up, axis, [(d, (d + 1) % ways) for d in range(ways)])
+        full = lax.dynamic_update_slice_in_dim(full, going_up, (here - far) % ways * hop, axis=dim)
+        if 2 * far < ways:
+            going_down = lax.ppermute(going_down, axis, [(d, (d - 1) % ways) for d in range(ways)])
+            full = lax.dynamic_update_slice_in_dim(
+                full, going_down, (here + far) % ways * hop, axis=dim
+            )
+    return full
 
 
 def with_halo(block, sides, width):
@@ -38,7 +54,7 @@
 def per_device(start_panel, tile_values, tile_column, tile_count):
 
     def fetch_owner(panel_part):
-        return lax.all_gather(panel_part, "cols", axis=1, tiled=True)
+        return gather_around(panel_part, "cols", 1)
 
     def partial_of(owner_panel):
         extended = with_halo(owner_panel, (("rows", 1),), owner_panel.shape[1])

time: 584 us -> 596 us (1.021); the launches traced: 583 us -> 588 us
  blocking collectives: 165 us -> 119 us
  waiting for transfers between devices: 260 us -> 296 us
  starting transfers between devices: 35.4 us -> 45.2 us
    ppermute x6, waiting for transfers between devices: 59.4 us -> 0.02 us  [with_halo(): lax.ppermute(lax.slice_in_dim(block, 0, width, axis=dim), axis, backward)]
    ppermute x6, waiting for transfers between devices: 66.9 us -> 118 us  [with_halo(): lax.ppermute(lax.slice_in_dim(block, block.shape[dim] - width, None, axis...]
    all_gather x6 -> x0, blocking collectives: 45.6 us -> none  [fetch_owner(): return lax.all_gather(panel_part, 'cols', axis=1, tiled=True)]
    ppermute x0 -> x18, waiting for transfers between devices: none -> 37.4 us  [the longest x12 37.4 us: gather_around(): lax.ppermute(going_up, axis, [(d, (d + 1) % ways) for d in range(ways)])]
    ppermute x0 -> x18, starting transfers between devices: none -> 15.1 us  [the longest x6 10.6 us: gather_around(): lax.ppermute(going_down, axis, [(d, (d - 1) % ways) for d in range(ways)])]
    reduce_scatter x6, waiting for transfers between devices: 133 us -> 141 us  [reduce_share(): lax.psum_scatter(partial_terms, 'cols', scatter_dimension=1, tiled=True)]
  transfers between devices with their start and end apart: 18 -> 36, of which waited for: 18 -> 24; matrix products, arithmetic and copies ran while one was open for 0% -> 1% of each run, Pallas kernels for 0% -> 0%
where the time goes in v1:
time: 596 us; the launch traced here: 588 us
  waiting for transfers between devices  296 us (50%)
  blocking collectives  119 us (20%)
  matrix products  52.7 us (9%)
  starting transfers between devices  45.2 us (8%)
  other arithmetic  38.8 us (7%)
  local copies, waits for them, and re-layouts  22 us (4%)
  between operations  14.3 us (2%)
    reduce_scatter x6, waiting for transfers between devices, reduce_share(): lax.psum_scatter(partial_terms, 'cols', scatter_dimension=1, tiled=True)  141 us
    psum x3, blocking collectives, per_device(): lower_factor = jnp.linalg.cholesky(lax.psum(local_gram, ('rows', 'cols')))  119 us
    ppermute x6, waiting for transfers between devices, with_halo(): lax.ppermute(lax.slice_in_dim(block, block.shape[dim] - width, None, axis...  118 us
    dot_general x6, matrix products, local_product(): jnp.einsum('disk,isnk->din', picked, tile_values, precision=lax.Precision...  44.6 us
    ppermute x12, waiting for transfers between devices, gather_around(): lax.ppermute(going_up, axis, [(d, (d + 1) % ways) for d in range(ways)])  37.4 us
    ppermute x6, starting transfers between devices, with_halo(): lax.ppermute(lax.slice_in_dim(block, block.shape[dim] - width, None, axis...  22.2 us
    another operation x9, other arithmetic, per_device(): lower_factor = jnp.linalg.cholesky(lax.psum(local_gram, ('rows', 'cols')))  19.6 us
    another operation x6, other arithmetic, per_device(): lax.linalg.triangular_solve(lower_factor, second, left_side=True, lower=T...  16.6 us
  transfers between devices with their start and end apart: 36, of which 24 were waited for; matrix products, arithmetic and copies ran while one was open for 1% of the time, Pallas kernels for 0%

profile of v1, /device:TPU:0, one launch (start us, length us, event | category | flops | bytes accessed | tf_op | source)
XLA Modules:
  0.0 588.3 jit_solution(4582196962419734332)
XLA Ops:
  13.3 2.9 collective-permute-done.2
  16.2 4.3 collective-permute-start.3
  23.5 19.3 %collective-permute-done.3 = f32[64,2048]{1,0:T(8,128)S(1)} collective-permute-done((f32[64,2048]{1,0:T(8,128)S(1)}, f32[64,2048]{1,0:T(8,128)S(1)}, u32[]{:S(2)}, u32[]{:S(2)}) %collective-permute-start.3) | collective-permute-done | bytes 524320 | tf_op jit(solution)/shard_map/ppermute | solution.py:31
  45.0 7.4 %fusion.12 = f32[16,8,8,128]{3,2,1,0:T(8,128)S(1)} fusion(f32[16,4,128,128]{3,2,1,0:T(8,128)} %param.10, f32[16,4,64,128]{3,2,1,0:T(8,128)} %bitcast.167, pred[16,4]{1,0:T(8,128)(4,1)S(1)} %copy.47, pred[16,4]{1,0:T(8,128)(4,1)S(1)} %broadcast_compare_fusion), kind=kOutput, calls=%fused_computation.36 | convolution fusion | flops 806354944 | bytes 6815872 | tf_op jit(solution)/shard_map/disk,isnk->din/dot_general | solution.py:50
  53.3 23.0 %reduce-scatter.7.cloned.1.call-done = f32[64,512]{1,0:T(8,128)} async-done(((f32[64,2048]{1,0:T(8,128)}), f32[64,512]{1,0:T(8,128)}) %reduce-scatter.7.cloned.1.call-update) | async-done | bytes 131088 | tf_op jit(solution)/shard_map/reduce_scatter | solution.py:64
  79.1 2.7 collective-permute-done.5
  81.8 4.3 collective-permute-done.7
  86.2 3.1 collective-permute-start.8
  90.6 18.9 %collective-permute-done.8 = f32[64,2048]{1,0:T(8,128)S(1)} collective-permute-done((f32[64,2048]{1,0:T(8,128)S(1)}, f32[64,2048]{1,0:T(8,128)S(1)}, u32[]{:S(2)}, u32[]{:S(2)}) %collective-permute-start.8) | collective-permute-done | bytes 524320 | tf_op jit(solution)/shard_map/ppermute | solution.py:31
  109.7 2.0 gather_fusion.1
  111.8 7.4 %fusion.13 = f32[16,8,8,128]{3,2,1,0:T(8,128)S(1)} fusion(f32[16,4,128,128]{3,2,1,0:T(8,128)} %param.10, f32[16,4,64,128]{3,2,1,0:T(8,128)} %bitcast.168, pred[16,4]{1,0:T(8,128)(4,1)S(1)} %copy.47, pred[16,4]{1,0:T(8,128)(4,1)S(1)} %broadcast_compare_fusion), kind=kOutput, calls=%fused_computation.37 | convolution fusion | flops 806354944 | bytes 6815872 | tf_op jit(solution)/shard_map/disk,isnk->din/dot_general | solution.py:50
  120.1 24.2 %reduce-scatter.9.cloned.1.call-done = f32[64,512]{1,0:T(8,128)} async-done(((f32[64,2048]{1,0:T(8,128)}), f32[64,512]{1,0:T(8,128)}) %reduce-scatter.9.cloned.1.call-update) | async-done | bytes 131088 | tf_op jit(solution)/shard_map/reduce_scatter | solution.py:64
  145.6 40.0 %psum.21 = f32[64,64]{0,1:T(8,128)S(1)} all-reduce(f32[64,64]{0,1:T(8,128)S(1)} %fusion.69), channel_id=1, replica_groups=mesh['rows'=8,'cols'=4] {'rows','cols'}, use_global_device_ids=true, to_apply=%region_2.4 | all-reduce | flops 4096 | bytes 32768 | tf_op jit(solution)/shard_map/psum | solution.py:74
  185.7 5.8 cholesky.59
  192.9 4.9 custom-call.7
  200.8 2.6 collective-permute-done.10
  204.8 3.1 collective-permute-done.12
  207.9 4.2 collective-permute-start.13
  213.4 21.0 %collective-permute-done.13 = f32[64,2048]{1,0:T(8,128)S(1)} collective-permute-done((f32[64,2048]{1,0:T(8,128)S(1)}, f32[64,2048]{1,0:T(8,128)S(1)}, u32[]{:S(2)}, u32[]{:S(2)}) %collective-permute-start.13) | collective-permute-done | bytes 524320 | tf_op jit(solution)/shard_map/ppermute | solution.py:31
  234.6 2.0 gather_fusion.2
  236.7 7.4 %fusion.14 = f32[16,8,8,128]{3,2,1,0:T(8,128)S(1)} fusion(f32[16,4,128,128]{3,2,1,0:T(8,128)} %param.10, f32[16,4,64,128]{3,2,1,0:T(8,128)} %bitcast.169, pred[16,4]{1,0:T(8,128)(4,1)S(1)} %copy.47, pred[16,4]{1,0:T(8,128)(4,1)S(1)} %broadcast_compare_fusion), kind=kOutput, calls=%fused_computation.38 | convolution fusion | flops 806354944 | bytes 6815872 | tf_op jit(solution)/shard_map/disk,isnk->din/dot_general | solution.py:50
  245.0 22.4 %reduce-scatter.11.cloned.1.call-done = f32[64,512]{1,0:T(8,128)} async-done(((f32[64,2048]{1,0:T(8,128)}), f32[64,512]{1,0:T(8,128)}) %reduce-scatter.11.cloned.1.call-update) | async-done | bytes 131088 | tf_op jit(solution)/shard_map/reduce_scatter | solution.py:64
  270.1 2.7 collective-permute-done.15
  272.9 4.3 collective-permute-done.17
  277.2 3.2 collective-permute-start.18
  281.7 18.8 %collective-permute-done.18 = f32[64,2048]{1,0:T(8,128)S(1)} collective-permute-done((f32[64,2048]{1,0:T(8,128)S(1)}, f32[64,2048]{1,0:T(8,128)S(1)}, u32[]{:S(2)}, u32[]{:S(2)}) %collective-permute-start.18) | collective-permute-done | bytes 524320 | tf_op jit(solution)/shard_map/ppermute | solution.py:31
  300.8 2.0 gather_fusion.3
  302.8 7.4 %fusion.15 = f32[16,8,8,128]{3,2,1,0:T(8,128)S(1)} fusion(f32[16,4,128,128]{3,2,1,0:T(8,128)} %param.10, f32[16,4,64,128]{3,2,1,0:T(8,128)} %bitcast.170, pred[16,4]{1,0:T(8,128)(4,1)S(1)} %copy.47, pred[16,4]{1,0:T(8,128)(4,1)S(1)} %broadcast_compare_fusion), kind=kOutput, calls=%fused_computation.39 | convolution fusion | flops 806354944 | bytes 6815872 | tf_op jit(solution)/shard_map/disk,isnk->din/dot_general | solution.py:50
  311.1 24.2 %reduce-scatter.13.cloned.1.call-done = f32[64,512]{1,0:T(8,128)} async-done(((f32[64,2048]{1,0:T(8,128)}), f32[64,512]{1,0:T(8,128)}) %reduce-scatter.13.cloned.1.call-update) | async-done | bytes 131088 | tf_op jit(solution)/shard_map/reduce_scatter | solution.py:64
  336.6 39.7 %psum.22 = f32[64,64]{0,1:T(8,128)S(1)} all-reduce(f32[64,64]{0,1:T(8,128)S(1)} %fusion.70), channel_id=1, replica_groups=mesh['rows'=8,'cols'=4] {'rows','cols'}, use_global_device_ids=true, to_apply=%region_7.11 | all-reduce | flops 4096 | bytes 32768 | tf_op jit(solution)/shard_map/psum | solution.py:74
  376.4 5.8 cholesky.70
  383.6 4.9 custom-call.8
  391.6 2.6 collective-permute-done.20
  395.5 3.1 collective-permute-done.22
  398.6 4.2 collective-permute-start.23
  404.2 21.0 %collective-permute-done.23 = f32[64,2048]{1,0:T(8,128)S(1)} collective-permute-done((f32[64,2048]{1,0:T(8,128)S(1)}, f32[64,2048]{1,0:T(8,128)S(1)}, u32[]{:S(2)}, u32[]{:S(2)}) %collective-permute-start.23) | collective-permute-done | bytes 524320 | tf_op jit(solution)/shard_map/ppermute | solution.py:31
  425.4 2.0 gather_fusion.4
  427.4 7.4 %fusion.16 = f32[16,8,8,128]{3,2,1,0:T(8,128)S(1)} fusion(f32[16,4,128,128]{3,2,1,0:T(8,128)} %param.10, f32[16,4,64,128]{3,2,1,0:T(8,128)} %bitcast.171, pred[16,4]{1,0:T(8,128)(4,1)S(1)} %copy.47, pred[16,4]{1,0:T(8,128)(4,1)S(1)} %broadcast_compare_fusion), kind=kOutput, calls=%fused_computation.40 | convolution fusion | flops 806354944 | bytes 6815872 | tf_op jit(solution)/shard_map/disk,isnk->din/dot_general | solution.py:50
  435.8 22.4 %reduce-scatter.15.cloned.1.call-done = f32[64,512]{1,0:T(8,128)} async-done(((f32[64,2048]{1,0:T(8,128)}), f32[64,512]{1,0:T(8,128)}) %reduce-scatter.15.cloned.1.call-update) | async-done | bytes 131088 | tf_op jit(solution)/shard_map/reduce_scatter | solution.py:64
  460.9 2.7 collective-permute-done.25
  463.6 4.3 collective-permute-done.27
  468.0 3.2 collective-permute-start.28
  472.5 18.9 %collective-permute-done.28 = f32[64,2048]{1,0:T(8,128)S(1)} collective-permute-done((f32[64,2048]{1,0:T(8,128)S(1)}, f32[64,2048]{1,0:T(8,128)S(1)}, u32[]{:S(2)}, u32[]{:S(2)}) %collective-permute-start.28) | collective-permute-done | bytes 524320 | tf_op jit(solution)/shard_map/ppermute | solution.py:31
  493.6 7.4 %fusion.17 = f32[16,8,8,128]{3,2,1,0:T(8,128)S(1)} fusion(f32[16,4,128,128]{3,2,1,0:T(8,128)} %param.10, f32[16,4,64,128]{3,2,1,0:T(8,128)} %bitcast.166, pred[16,4]{1,0:T(8,128)(4,1)S(1)} %copy.47, pred[16,4]{1,0:T(8,128)(4,1)S(1)} %broadcast_compare_fusion), kind=kOutput, calls=%fused_computation.41 | convolution fusion | flops 806354944 | bytes 6815872 | tf_op jit(solution)/shard_map/disk,isnk->din/dot_general | solution.py:50
  501.9 24.3 %reduce-scatter.17.cloned.1.call-done = f32[64,512]{1,0:T(8,128)} async-done(((f32[64,2048]{1,0:T(8,128)}), f32[64,512]{1,0:T(8,128)}) %reduce-scatter.17.cloned.1.call-update) | async-done | bytes 131088 | tf_op jit(solution)/shard_map/reduce_scatter | solution.py:64
  527.4 39.7 %psum.23 = f32[64,64]{0,1:T(8,128)S(1)} all-reduce(f32[64,64]{0,1:T(8,128)S(1)} %fusion.71), channel_id=1, replica_groups=mesh['rows'=8,'cols'=4] {'rows','cols'}, use_global_device_ids=true, to_apply=%region_10.14 | all-reduce | flops 4096 | bytes 32768 | tf_op jit(solution)/shard_map/psum | solution.py:74
  567.2 5.8 cholesky.81
  574.4 4.9 custom-call.9
  (119 shorter events, 53.5 us)
Async XLA Ops:
  6.5 69.8 %reduce-scatter.7.cloned.1.call-start = ((), (), s32[]{:S(2)}) async-start(), calls=%async_computation.6 | async-start | bytes 655360 | tf_op jit(solution)/shard_map/reduce_scatter | solution.py:64
  6.5 5.2 collective-permute-start
  7.0 6.2 %collective-permute-start.1 = (f32[64,512]{1,0:T(8,128)}, f32[64,512]{1,0:T(8,128)S(1)}, u32[]{:S(2)}, u32[]{:S(2)}) collective-permute-start(f32[64,512]{1,0:T(8,128)} %param.9), channel_id=1, source_target_pairs={{0,3},{1,0},{2,1},{3,2},{4,7},{5,4},{6,5},{7,6},{8,11},{9,8},{10,9... | collective-permute-start | bytes 393224 | tf_op jit(solution)/shard_map/ppermute | solution.py:19
  11.8 4.4 collective-permute-start.2
  16.2 26.6 %collective-permute-start.3 = (f32[64,2048]{1,0:T(8,128)S(1)}, f32[64,2048]{1,0:T(8,128)S(1)}, u32[]{:S(2)}, u32[]{:S(2)}) collective-permute-start(f32[64,2048]{1,0:T(8,128)S(1)} %constant_dynamic-update-slice_fusion.20), channel_id=1, source_target_pairs={{0,4},{4,8},{8,12},{12,16},{16,20},{20,24},{24,28},{1,5},{5,9},{9,... | collective-permute-start | bytes 1572872 | tf_op jit(solution)/shard_map/ppermute | solution.py:31
  20.5 22.3 %collective-permute-start.4 = (f32[64,2048]{1,0:T(8,128)S(1)}, f32[64,2048]{1,0:T(8,128)S(1)}, u32[]{:S(2)}, u32[]{:S(2)}) collective-permute-start(f32[64,2048]{1,0:T(8,128)S(1)} %constant_dynamic-update-slice_fusion.20), channel_id=1, source_target_pairs={{4,0},{8,4},{12,8},{16,12},{20,16},{24,20},{28,24},{5,1},{9,5},{13... | collective-permute-start | bytes 1572872 | tf_op jit(solution)/shard_map/ppermute | solution.py:34
  53.3 91.1 %reduce-scatter.9.cloned.1.call-start = ((), (), s32[]{:S(2)}) async-start(), calls=%async_computation.7 | async-start | bytes 655360 | tf_op jit(solution)/shard_map/reduce_scatter | solution.py:64
  76.3 5.4 collective-permute-start.5
  76.3 5.5 collective-permute-start.6
  81.8 4.4 collective-permute-start.7
  86.2 23.3 %collective-permute-start.8 = (f32[64,2048]{1,0:T(8,128)S(1)}, f32[64,2048]{1,0:T(8,128)S(1)}, u32[]{:S(2)}, u32[]{:S(2)}) collective-permute-start(f32[64,2048]{1,0:T(8,128)S(1)} %constant_dynamic-update-slice_fusion.16), channel_id=1, source_target_pairs={{0,4},{4,8},{8,12},{12,16},{16,20},{20,24},{24,28},{1,5},{5,9},{9,... | collective-permute-start | bytes 1572872 | tf_op jit(solution)/shard_map/ppermute | solution.py:31
  89.3 20.2 %collective-permute-start.9 = (f32[64,2048]{1,0:T(8,128)S(1)}, f32[64,2048]{1,0:T(8,128)S(1)}, u32[]{:S(2)}, u32[]{:S(2)}) collective-permute-start(f32[64,2048]{1,0:T(8,128)S(1)} %constant_dynamic-update-slice_fusion.16), channel_id=1, source_target_pairs={{4,0},{8,4},{12,8},{16,12},{20,16},{24,20},{28,24},{5,1},{9,5},{13... | collective-permute-start | bytes 1572872 | tf_op jit(solution)/shard_map/ppermute | solution.py:34
  120.1 147.3 %reduce-scatter.11.cloned.1.call-start = ((), (), s32[]{:S(2)}) async-start(), calls=%async_computation.8 | async-start | bytes 655360 | tf_op jit(solution)/shard_map/reduce_scatter | solution.py:64
  199.0 4.4 collective-permute-start.10
  199.1 5.6 collective-permute-start.11
  203.5 4.4 collective-permute-start.12
  207.9 26.5 %collective-permute-start.13 = (f32[64,2048]{1,0:T(8,128)S(1)}, f32[64,2048]{1,0:T(8,128)S(1)}, u32[]{:S(2)}, u32[]{:S(2)}) collective-permute-start(f32[64,2048]{1,0:T(8,128)S(1)} %constant_dynamic-update-slice_fusion.12), channel_id=1, source_target_pairs={{0,4},{4,8},{8,12},{12,16},{16,20},{20,24},{24,28},{1,5},{5,9},{9,... | collective-permute-start | bytes 1572872 | tf_op jit(solution)/shard_map/ppermute | solution.py:31
  212.1 22.3 %collective-permute-start.14 = (f32[64,2048]{1,0:T(8,128)S(1)}, f32[64,2048]{1,0:T(8,128)S(1)}, u32[]{:S(2)}, u32[]{:S(2)}) collective-permute-start(f32[64,2048]{1,0:T(8,128)S(1)} %constant_dynamic-update-slice_fusion.12), channel_id=1, source_target_pairs={{4,0},{8,4},{12,8},{16,12},{20,16},{24,20},{28,24},{5,1},{9,5},{13... | collective-permute-start | bytes 1572872 | tf_op jit(solution)/shard_map/ppermute | solution.py:34
  245.0 90.4 %reduce-scatter.13.cloned.1.call-start = ((), (), s32[]{:S(2)}) async-start(), calls=%async_computation.9 | async-start | bytes 655360 | tf_op jit(solution)/shard_map/reduce_scatter | solution.py:64
  267.4 5.4 collective-permute-start.15
  267.4 5.5 collective-permute-start.16
  272.8 4.4 collective-permute-start.17
  277.2 23.3 %collective-permute-start.18 = (f32[64,2048]{1,0:T(8,128)S(1)}, f32[64,2048]{1,0:T(8,128)S(1)}, u32[]{:S(2)}, u32[]{:S(2)}) collective-permute-start(f32[64,2048]{1,0:T(8,128)S(1)} %constant_dynamic-update-slice_fusion.8), channel_id=1, source_target_pairs={{0,4},{4,8},{8,12},{12,16},{16,20},{20,24},{24,28},{1,5},{5,9},{9,... | collective-permute-start | bytes 1572872 | tf_op jit(solution)/shard_map/ppermute | solution.py:31
  280.4 20.2 %collective-permute-start.19 = (f32[64,2048]{1,0:T(8,128)S(1)}, f32[64,2048]{1,0:T(8,128)S(1)}, u32[]{:S(2)}, u32[]{:S(2)}) collective-permute-start(f32[64,2048]{1,0:T(8,128)S(1)} %constant_dynamic-update-slice_fusion.8), channel_id=1, source_target_pairs={{4,0},{8,4},{12,8},{16,12},{20,16},{24,20},{28,24},{5,1},{9,5},{13... | collective-permute-start | bytes 1572872 | tf_op jit(solution)/shard_map/ppermute | solution.py:34
  311.1 147.0 %reduce-scatter.15.cloned.1.call-start = ((), (), s32[]{:S(2)}) async-start(), calls=%async_computation.10 | async-start | bytes 655360 | tf_op jit(solution)/shard_map/reduce_scatter | solution.py:64
  389.8 4.4 collective-permute-start.20
  389.9 5.6 collective-permute-start.21
  394.2 4.4 collective-permute-start.22
  398.6 26.5 %collective-permute-start.23 = (f32[64,2048]{1,0:T(8,128)S(1)}, f32[64,2048]{1,0:T(8,128)S(1)}, u32[]{:S(2)}, u32[]{:S(2)}) collective-permute-start(f32[64,2048]{1,0:T(8,128)S(1)} %constant_dynamic-update-slice_fusion.4), channel_id=1, source_target_pairs={{0,4},{4,8},{8,12},{12,16},{16,20},{20,24},{24,28},{1,5},{5,9},{9,... | collective-permute-start | bytes 1572872 | tf_op jit(solution)/shard_map/ppermute | solution.py:31
  402.9 22.3 %collective-permute-start.24 = (f32[64,2048]{1,0:T(8,128)S(1)}, f32[64,2048]{1,0:T(8,128)S(1)}, u32[]{:S(2)}, u32[]{:S(2)}) collective-permute-start(f32[64,2048]{1,0:T(8,128)S(1)} %constant_dynamic-update-slice_fusion.4), channel_id=1, source_target_pairs={{4,0},{8,4},{12,8},{16,12},{20,16},{24,20},{28,24},{5,1},{9,5},{13... | collective-permute-start | bytes 1572872 | tf_op jit(solution)/shard_map/ppermute | solution.py:34
  435.7 90.4 %reduce-scatter.17.cloned.1.call-start = ((), (), s32[]{:S(2)}) async-start(), calls=%async_computation.11 | async-start | bytes 655360 | tf_op jit(solution)/shard_map/reduce_scatter | solution.py:64
  458.1 5.4 collective-permute-start.25
  458.1 5.5 collective-permute-start.26
  463.6 4.4 collective-permute-start.27
  468.0 23.3 %collective-permute-start.28 = (f32[64,2048]{1,0:T(8,128)S(1)}, f32[64,2048]{1,0:T(8,128)S(1)}, u32[]{:S(2)}, u32[]{:S(2)}) collective-permute-start(f32[64,2048]{1,0:T(8,128)S(1)} %constant_dynamic-update-slice_fusion), channel_id=1, source_target_pairs={{0,4},{4,8},{8,12},{12,16},{16,20},{20,24},{24,28},{1,5},{5,9},{9,... | collective-permute-start | bytes 1572872 | tf_op jit(solution)/shard_map/ppermute | solution.py:31
  471.2 20.2 %collective-permute-start.29 = (f32[64,2048]{1,0:T(8,128)S(1)}, f32[64,2048]{1,0:T(8,128)S(1)}, u32[]{:S(2)}, u32[]{:S(2)}) collective-permute-start(f32[64,2048]{1,0:T(8,128)S(1)} %constant_dynamic-update-slice_fusion), channel_id=1, source_target_pairs={{4,0},{8,4},{12,8},{16,12},{20,16},{24,20},{28,24},{5,1},{9,5},{13... | collective-permute-start | bytes 1572872 | tf_op jit(solution)/shard_map/ppermute | solution.py:34
Sparse Core Ops, SparseCore 0:
  53.4 22.8 reduce-scatter.6
  120.2 24.1 reduce-scatter.8
  245.1 22.2 reduce-scatter.10
  311.2 24.1 reduce-scatter.12
  435.8 22.2 reduce-scatter.14
  502.0 24.1 reduce-scatter.16
